TPU v7x, 256 devices: a whole 4x4x8 slice. The times are simulated.
256 devices in a mesh: shard: 16 (over z, core), tensor: 4 (over x), section: 4 (over y).
Axes of the slice: x: 4, y: 4, z: 8, core: 2. Of those that a mesh axis runs over, the one named last changes fastest.
Arguments:
- gradient: bfloat16 [6, 2048, 8192], P(None, ('tensor', 'section'), 'shard'), may hold values from -6 to 6
- basis: bfloat16 [6, 2048, 256], P(None, ('tensor', 'section')), may hold values from -6 to 6
- moment_m: float32 [6, 8192, 256], P(None, ('shard', 'tensor', 'section')), may hold values from -4 to 4
- moment_v: float32 [6, 8192, 256], P(None, ('shard', 'tensor', 'section')), may hold values from 0.002 to 0.02
Outputs:
- delta: bfloat16 [6, 2048, 8192], P(None, ('tensor', 'section'), 'shard')
- basis_new: bfloat16 [6, 2048, 256], P(None, ('tensor', 'section'))
- moment_m_new: float32 [6, 8192, 256], P(None, ('shard', 'tensor', 'section'))
- moment_v_new: float32 [6, 8192, 256], P(None, ('shard', 'tensor', 'section'))
All inputs are finite; a program needn't handle non-finite values. Where the computation divides by a largest or mean magnitude, that divisor is 1e-20 or more.
Results may differ from a plain program's by a relative error of at most 0.0049.
Values may be sent and summed in bfloat16 or wider, within the bound.
A program may use at most 64 MiB of HBM per device.

v0:
```python
import math
import jax
import jax.numpy as jnp
from jax import lax
from jax.sharding import PartitionSpec as P

D = 2048
NS_ITERS = 4
beta_one = 0.9
beta_two = 0.999
bias_one = 1.0 - 0.9**10
bias_two = 1.0 - 0.999**10
eps_adam = 1e-08
galore_gain = 4.0


def gram_total(iterate):
    local_gram = jnp.einsum("kmr,kms->krs", iterate, iterate, precision=lax.Precision.HIGHEST)
    return lax.psum(local_gram, ("tensor", "section"))


def orthogonal(subspace):
    gram_mat = gram_total(subspace)
    row_bound = jnp.max(jnp.sum(jnp.abs(gram_mat), axis=2), axis=1)[:, None, None] + 1e-06
    iterate = subspace / jnp.sqrt(row_bound)
    gram_mat = gram_mat / row_bound
    identity = jnp.eye(gram_mat.shape[1], dtype=jnp.float32)
    for turn_index in range(NS_ITERS):
        factor = 1.5 * identity - 0.5 * gram_mat
        iterate = jnp.einsum("kmr,krs->kms", iterate, factor, precision=lax.Precision.HIGHEST)
        if turn_index + 1 < NS_ITERS:
            gram_mat = gram_total(iterate)
    return iterate


def per_device(gradient, basis, moment_m, moment_v):
    width_root = math.sqrt(D)
    partial_low = jnp.einsum("kmn,kmr->knr", gradient, basis, preferred_element_type=jnp.float32)
    low_rank = (
        lax.psum_scatter(partial_low, ("tensor", "section"), scatter_dimension=1, tiled=True)
        / width_root
    )
    moment_m_new = beta_one * moment_m + (1.0 - beta_one) * low_rank
    moment_v_new = beta_two * moment_v + (1.0 - beta_two) * low_rank * low_rank
    step_low = (moment_m_new / bias_one / (jnp.sqrt(moment_v_new / bias_two) + eps_adam)).astype(
        jnp.bfloat16
    )
    rough_low = low_rank.astype(jnp.bfloat16)
    step_block, rough_block = (
        lax.all_gather(step_low, ("tensor", "section"), axis=1, tiled=True),
        lax.all_gather(rough_low, ("tensor", "section"), axis=1, tiled=True),
    )
    delta = (
        -galore_gain
        / width_root
        * jnp.einsum("kmr,knr->kmn", basis, step_block, preferred_element_type=jnp.float32)
    ).astype(jnp.bfloat16)
    subspace = jnp.einsum("kmn,knr->kmr", gradient, rough_block, preferred_element_type=jnp.float32)
    whole_sum = lax.psum(subspace, "shard")
    basis_new = (width_root * orthogonal(whole_sum)).astype(jnp.bfloat16)
    return (delta, basis_new, moment_m_new, moment_v_new)


def solution(mesh):
    placed = (
        P(None, ("tensor", "section"), "shard"),
        P(None, ("tensor", "section"), None),
        P(None, ("shard", "tensor", "section"), None),
        P(None, ("shard", "tensor", "section"), None),
    )
    return jax.shard_map(
        per_device,
        mesh=mesh,
        in_specs=placed,
        out_specs=(
            P(None, ("tensor", "section"), "shard"),
            P(None, ("tensor", "section"), None),
            P(None, ("shard", "tensor", "section"), None),
            P(None, ("shard", "tensor", "section"), None),
        ),
        check_vma=False,
    )
```

profile of v0, /device:TPU:32, one launch (start us, length us, event | category | flops | bytes accessed | tf_op | source)
XLA Modules:
  0.0 738.4 jit_solution(1374766177256162602)
XLA Ops:
  7.2 1.1 copy-done
  8.3 3.3 fusion.37
  11.6 84.4 %reduce-scatter.2.cloned.1.call-done = f32[6,32,256]{2,1,0:T(8,128)} async-done(((f32[6,512,256]{2,1,0:T(8,128)}), f32[6,32,256]{2,1,0:T(8,128)}) %reduce-scatter.2.cloned.1.call-update) | async-done | bytes 196624 | tf_op jit(solution)/shard_map/reduce_scatter | solution.py:40
  96.0 1.8 divide_convert_fusion
  97.9 49.2 %all-gather.5.cloned.1.call-done = bf16[6,512,256]{2,1,0:T(8,128)(2,1)} async-done(((bf16[6,32,256]{2,1,0:T(8,128)(2,1)}), bf16[6,512,256]{2,1,0:T(8,128)(2,1)}) %all-gather.5.cloned.1.call-update) | async-done | bytes 1572880 | tf_op jit(solution)/shard_map/all_gather | solution.py:51
  147.2 2.9 convolution_bitcast_fusion
  150.2 108.3 %all-reduce.6.cloned.1.call-done = f32[6,128,256]{1,2,0:T(8,128)} async-done(((f32[6,128,256]{1,2,0:T(8,128)}), f32[6,128,256]{1,2,0:T(8,128)}) %all-reduce.6.cloned.1.call-update) | async-done | bytes 786448 | tf_op jit(solution)/shard_map/psum | solution.py:59
  258.5 3.9 fusion.38
  262.5 102.3 %all-reduce.8.cloned.1.call-done = f32[6,256,256]{2,1,0:T(8,128)} async-done(((f32[6,256,256]{2,1,0:T(8,128)}), f32[6,256,256]{2,1,0:T(8,128)}) %all-reduce.8.cloned.1.call-update) | async-done | bytes 1572880 | tf_op jit(solution)/shard_map/psum | solution.py:19
  364.8 1.7 abs_reduce_fusion
  366.6 3.2 fusion.9
  369.8 2.6 fusion.39
  372.5 98.7 %all-reduce.10.cloned.1.call-done = f32[6,256,256]{2,1,0:T(8,128)} async-done(((f32[6,256,256]{2,1,0:T(8,128)}), f32[6,256,256]{2,1,0:T(8,128)}) %all-reduce.10.cloned.1.call-update) | async-done | bytes 1572880 | tf_op jit(solution)/shard_map/psum | solution.py:19
  471.1 2.6 fusion.6
  473.7 2.6 fusion.40
  476.4 0.7 all-gather.3.cloned.1.call-update
  477.3 97.7 %all-reduce.12.cloned.1.call-done = f32[6,256,256]{2,1,0:T(8,128)} async-done(((f32[6,256,256]{2,1,0:T(8,128)}), f32[6,256,256]{2,1,0:T(8,128)}) %all-reduce.12.cloned.1.call-update) | async-done | bytes 1572880 | tf_op jit(solution)/shard_map/psum | solution.py:19
  575.1 2.6 fusion.3
  577.6 2.6 fusion.41
  580.3 46.1 %all-gather.3.cloned.1.call-done = bf16[6,512,256]{2,1,0:T(8,128)(2,1)} async-done(((bf16[6,32,256]{2,1,0:T(8,128)(2,1)}), bf16[6,512,256]{2,1,0:T(8,128)(2,1)}) %all-gather.3.cloned.1.call-update) | async-done | bytes 1572880 | tf_op jit(solution)/shard_map/all_gather | solution.py:50
  626.4 2.0 fusion.13
  628.3 1.2 copy.15
  629.5 98.7 %all-reduce.14.cloned.1.call-done = f32[6,256,256]{2,1,0:T(8,128)} async-done(((f32[6,256,256]{2,1,0:T(8,128)}), f32[6,256,256]{2,1,0:T(8,128)}) %all-reduce.14.cloned.1.call-update) | async-done | bytes 1572880 | tf_op jit(solution)/shard_map/psum | solution.py:19
  728.2 3.3 fusion.17
  (27 shorter events, 0.8 us)
Async XLA Ops:
  7.2 1.1 copy-start
  7.2 88.8 %reduce-scatter.2.cloned.1.call-start = ((), (), s32[]{:S(2)}) async-start(), calls=%async_computation.1 | async-start | bytes 3342336 | tf_op jit(solution)/shard_map/reduce_scatter | solution.py:40
  11.6 84.4 %copy-start.3 = (f32[6,32,256]{2,1,0:T(8,128)S(1)}, f32[6,32,256]{2,1,0:T(8,128)}, u32[]{:S(2)}) copy-start(f32[6,32,256]{2,1,0:T(8,128)} %param.6) | copy-start | bytes 589828
  11.6 84.4 %copy-start.4 = (f32[6,32,256]{2,1,0:T(8,128)S(1)}, f32[6,32,256]{2,1,0:T(8,128)}, u32[]{:S(2)}) copy-start(f32[6,32,256]{2,1,0:T(8,128)} %param.7) | copy-start | bytes 589828
  11.6 135.6 %all-gather.5.cloned.1.call-start = ((), (), s32[]{:S(2)}) async-start(), calls=%async_computation.3 | async-start | bytes 1671168 | tf_op jit(solution)/shard_map/all_gather | solution.py:51
  97.9 160.6 %all-reduce.6.cloned.1.call-start = ((), (), s32[]{:S(2)}) async-start(), calls=%async_computation.4 | async-start | bytes 1572864 | tf_op jit(solution)/shard_map/psum | solution.py:59
  150.1 214.7 %all-reduce.8.cloned.1.call-start = ((), (), s32[]{:S(2)}) async-start(), calls=%async_computation.5 | async-start | bytes 3145728 | tf_op jit(solution)/shard_map/psum | solution.py:19
  262.4 104.2 %copy-start.1 = (f32[6,128,256]{1,2,0:T(8,128)S(1)}, f32[6,128,256]{1,2,0:T(8,128)}, u32[]{:S(2)}) copy-start(f32[6,128,256]{1,2,0:T(8,128)} %all-reduce.6.cloned.1.call-done) | copy-start | bytes 2359300
  262.5 208.7 %all-reduce.10.cloned.1.call-start = ((), (), s32[]{:S(2)}) async-start(), calls=%async_computation.6 | async-start | bytes 3145728 | tf_op jit(solution)/shard_map/psum | solution.py:19
  372.4 202.6 %all-reduce.12.cloned.1.call-start = ((), (), s32[]{:S(2)}) async-start(), calls=%async_computation.7 | async-start | bytes 3145728 | tf_op jit(solution)/shard_map/psum | solution.py:19
  476.4 150.0 %all-gather.3.cloned.1.call-start = ((), (), s32[]{:S(2)}) async-start(), calls=%async_computation.2 | async-start | bytes 1671168 | tf_op jit(solution)/shard_map/all_gather | solution.py:50
  477.1 251.1 %all-reduce.14.cloned.1.call-start = ((), (), s32[]{:S(2)}) async-start(), calls=%async_computation.8 | async-start | bytes 3145728 | tf_op jit(solution)/shard_map/psum | solution.py:19
  580.3 46.1 %copy-start.2 = (bf16[6,128,256]{2,1,0:T(8,128)(2,1)S(1)}, bf16[6,128,256]{2,1,0:T(8,128)(2,1)}, u32[]{:S(2)}) copy-start(bf16[6,128,256]{2,1,0:T(8,128)(2,1)} %param.5) | copy-start | bytes 1179652
Sparse Core Ops, SparseCore 0:
  11.7 84.2 reduce-scatter.1
  99.1 48.0 all-gather.4
  150.2 108.2 all-reduce.5
  262.6 102.1 all-reduce.7
  372.6 98.5 all-reduce.9
  476.5 98.5 all-reduce.11
  578.1 48.1 all-gather.2
  629.7 98.5 all-reduce.13
where the time goes:
time: 739 us; the launch traced here: 738 us
  waiting for transfers between devices  686 us (93%)
  matrix products  31.6 us (4%)
  between operations  14.2 us (2%)
    psum x4, waiting for transfers between devices, gram_total(): return lax.psum(local_gram, ('tensor', 'section'))  397 us
    psum x1, waiting for transfers between devices, per_device(): whole_sum = lax.psum(subspace, 'shard')  108 us
    reduce_scatter x1, waiting for transfers between devices, per_device(): lax.psum_scatter(partial_low, ('tensor', 'section'), scatter_dimension=1,...  84.4 us
    all_gather x1, waiting for transfers between devices, per_device(): lax.all_gather(rough_low, ('tensor', 'section'), axis=1, tiled=True)  49.2 us
    all_gather x1, waiting for transfers between devices, per_device(): lax.all_gather(step_low, ('tensor', 'section'), axis=1, tiled=True)  46.1 us
  transfers between devices with their start and end apart: 8, of which 8 were waited for; matrix products, arithmetic and copies ran while one was open for 1% of the time, Pallas kernels for 0%

commit v1 on v0

--- a/solution.py
+++ b/solution.py
@@ -14,9 +14,15 @@
 galore_gain = 4.0
 
 
+def add_all(shard, mesh_axis):
+    pieces = lax.all_gather(shard, mesh_axis, axis=0, tiled=False)
+    acc = pieces.sum(axis=0)
+    return acc
+
+
 def gram_total(iterate):
     local_gram = jnp.einsum("kmr,kms->krs", iterate, iterate, precision=lax.Precision.HIGHEST)
-    return lax.psum(local_gram, ("tensor", "section"))
+    return add_all(local_gram, ("tensor", "section"))
 
 
 def orthogonal(subspace):

time: 739 us -> 1000 us (1.35)
  waiting for transfers between devices: 686 us -> 918 us
  other arithmetic: 3.66 us -> 39.5 us
    all_gather x0 -> x4, waiting for transfers between devices: none -> 637 us  [add_all(): pieces = lax.all_gather(shard, mesh_axis, axis=0, tiled=False)]
    psum x4 -> x0, waiting for transfers between devices: 397 us -> none  [gram_total(): return lax.psum(local_gram, ('tensor', 'section'))]
    reduce_sum x0 -> x4, other arithmetic: none -> 37.3 us  [add_all(): acc = pieces.sum(axis=0)]
  transfers between devices with their start and end apart: 8 -> 8, of which waited for: 8 -> 8; matrix products, arithmetic and copies ran while one was open for 1% -> 2% of each run, Pallas kernels for 0% -> 0%
where the time goes in v1:
time: 1000 us
  waiting for transfers between devices  918 us (92%)
  other arithmetic  39.5 us (4%)
  matrix products  26 us (3%)
  between operations  14.2 us (1%)
    all_gather x4, waiting for transfers between devices, add_all(): pieces = lax.all_gather(shard, mesh_axis, axis=0, tiled=False)  637 us
    psum x1, waiting for transfers between devices, per_device(): whole_sum = lax.psum(subspace, 'shard')  108 us
    reduce_scatter x1, waiting for transfers between devices, per_device(): lax.psum_scatter(partial_low, ('tensor', 'section'), scatter_dimension=1,...  84.3 us
    all_gather x1, waiting for transfers between devices, per_device(): lax.all_gather(rough_low, ('tensor', 'section'), axis=1, tiled=True)  49.3 us
    all_gather x1, waiting for transfers between devices, per_device(): lax.all_gather(step_low, ('tensor', 'section'), axis=1, tiled=True)  38.4 us
    reduce_sum x4, other arithmetic, add_all(): acc = pieces.sum(axis=0)  37.3 us
  transfers between devices with their start and end apart: 8, of which 8 were waited for; matrix products, arithmetic and copies ran while one was open for 2% of the time, Pallas kernels for 0%

profile of v1, /device:TPU:32, one launch (start us, length us, event | category | flops | bytes accessed | tf_op | source)
XLA Modules:
  0.0 1001.5 jit_solution(12645789667474293930)
XLA Ops:
  8.3 3.3 fusion.37
  11.6 84.3 %reduce-scatter.2.cloned.1.call-done = f32[6,32,256]{2,1,0:T(8,128)} async-done(((f32[6,512,256]{2,1,0:T(8,128)}), f32[6,32,256]{2,1,0:T(8,128)}) %reduce-scatter.2.cloned.1.call-update) | async-done | bytes 196624 | tf_op jit(solution)/shard_map/reduce_scatter | solution.py:46
  96.0 1.8 divide_convert_fusion
  97.9 49.3 %all-gather.13.cloned.1.call-done = bf16[6,512,256]{2,1,0:T(8,128)(2,1)} async-done(((bf16[6,32,256]{2,1,0:T(8,128)(2,1)}), bf16[6,512,256]{2,1,0:T(8,128)(2,1)}) %all-gather.13.cloned.1.call-update) | async-done | bytes 1572880 | tf_op jit(solution)/shard_map/all_gather | solution.py:57
  147.2 2.9 convolution_bitcast_fusion
  150.2 108.3 %all-reduce.2.cloned.1.call-done = f32[6,128,256]{1,2,0:T(8,128)} async-done(((f32[6,128,256]{1,2,0:T(8,128)}), f32[6,128,256]{1,2,0:T(8,128)}) %all-reduce.2.cloned.1.call-update) | async-done | bytes 786448 | tf_op jit(solution)/shard_map/psum | solution.py:65
  258.5 4.0 fusion.38
  262.6 162.2 %all-gather.15.cloned.1.call-done = f32[96,256,256]{2,1,0:T(8,128)} async-done(((f32[6,256,256]{2,1,0:T(8,128)}), f32[96,256,256]{2,1,0:T(8,128)}) %all-gather.15.cloned.1.call-update) | async-done | bytes 25165840 | tf_op jit(solution)/shard_map/all_gather | solution.py:18
  424.8 9.3 reduce_sum.45
  435.3 1.7 fusion.9
  437.0 2.7 fusion.39
  439.8 158.9 %all-gather.17.cloned.1.call-done = f32[96,256,256]{2,1,0:T(8,128)} async-done(((f32[6,256,256]{2,1,0:T(8,128)}), f32[96,256,256]{2,1,0:T(8,128)}) %all-gather.17.cloned.1.call-update) | async-done | bytes 25165840 | tf_op jit(solution)/shard_map/all_gather | solution.py:18
  598.7 9.3 reduce_sum.47
  609.2 2.6 fusion.40
  612.8 158.0 %all-gather.19.cloned.1.call-done = f32[96,256,256]{2,1,0:T(8,128)} async-done(((f32[6,256,256]{2,1,0:T(8,128)}), f32[96,256,256]{2,1,0:T(8,128)}) %all-gather.19.cloned.1.call-update) | async-done | bytes 25165840 | tf_op jit(solution)/shard_map/all_gather | solution.py:18
  770.8 9.3 reduce_sum.48
  780.2 1.2 fusion.3
  781.3 2.6 fusion.41
  784.0 38.4 %all-gather.11.cloned.1.call-done = bf16[6,512,256]{2,1,0:T(8,128)(2,1)} async-done(((bf16[6,32,256]{2,1,0:T(8,128)(2,1)}), bf16[6,512,256]{2,1,0:T(8,128)(2,1)}) %all-gather.11.cloned.1.call-update) | async-done | bytes 1572880 | tf_op jit(solution)/shard_map/all_gather | solution.py:56
  822.4 2.0 fusion.13
  824.4 1.2 copy.28
  825.5 157.9 %all-gather.21.cloned.1.call-done = f32[96,256,256]{2,1,0:T(8,128)} async-done(((f32[6,256,256]{2,1,0:T(8,128)}), f32[96,256,256]{2,1,0:T(8,128)}) %all-gather.21.cloned.1.call-update) | async-done | bytes 25165840 | tf_op jit(solution)/shard_map/all_gather | solution.py:18
  983.4 9.3 reduce_sum.49
  992.8 1.9 fusion.17
  (33 shorter events, 4.7 us)
Async XLA Ops:
  7.2 1.1 copy-start
  7.2 88.8 %reduce-scatter.2.cloned.1.call-start = ((), (), s32[]{:S(2)}) async-start(), calls=%async_computation.1 | async-start | bytes 3342336 | tf_op jit(solution)/shard_map/reduce_scatter | solution.py:46
  11.6 84.4 %copy-start.4 = (f32[6,32,256]{2,1,0:T(8,128)S(1)}, f32[6,32,256]{2,1,0:T(8,128)}, u32[]{:S(2)}) copy-start(f32[6,32,256]{2,1,0:T(8,128)} %param.6) | copy-start | bytes 589828
  11.6 84.4 %copy-start.5 = (f32[6,32,256]{2,1,0:T(8,128)S(1)}, f32[6,32,256]{2,1,0:T(8,128)}, u32[]{:S(2)}) copy-start(f32[6,32,256]{2,1,0:T(8,128)} %param.7) | copy-start | bytes 589828
  11.6 135.6 %all-gather.13.cloned.1.call-start = ((), (), s32[]{:S(2)}) async-start(), calls=%async_computation.3 | async-start | bytes 1671168 | tf_op jit(solution)/shard_map/all_gather | solution.py:57
  97.8 160.7 %all-reduce.2.cloned.1.call-start = ((), (), s32[]{:S(2)}) async-start(), calls=%async_computation.4 | async-start | bytes 1572864 | tf_op jit(solution)/shard_map/psum | solution.py:65
  150.1 274.7 %all-gather.15.cloned.1.call-start = ((), (), s32[]{:S(2)}) async-start(), calls=%async_computation.5 | async-start | bytes 26738688 | tf_op jit(solution)/shard_map/all_gather | solution.py:18
  262.5 336.2 %all-gather.17.cloned.1.call-start = ((), (), s32[]{:S(2)}) async-start(), calls=%async_computation.6 | async-start | bytes 26738688 | tf_op jit(solution)/shard_map/all_gather | solution.py:18
  434.1 1.1 copy-start.2
  439.7 331.1 %all-gather.19.cloned.1.call-start = ((), (), s32[]{:S(2)}) async-start(), calls=%async_computation.7 | async-start | bytes 26738688 | tf_op jit(solution)/shard_map/all_gather | solution.py:18
  611.8 210.5 %all-gather.11.cloned.1.call-start = ((), (), s32[]{:S(2)}) async-start(), calls=%async_computation.2 | async-start | bytes 1671168 | tf_op jit(solution)/shard_map/all_gather | solution.py:56
  612.6 370.8 %all-gather.21.cloned.1.call-start = ((), (), s32[]{:S(2)}) async-start(), calls=%async_computation.8 | async-start | bytes 26738688 | tf_op jit(solution)/shard_map/all_gather | solution.py:18
  783.9 38.5 %copy-start.3 = (bf16[6,128,256]{2,1,0:T(8,128)(2,1)S(1)}, bf16[6,128,256]{2,1,0:T(8,128)(2,1)}, u32[]{:S(2)}) copy-start(bf16[6,128,256]{2,1,0:T(8,128)(2,1)} %param.5) | copy-start | bytes 1179652
  983.4 11.3 %copy-start.1 = (bf16[6,128,512]{2,1,0:T(8,128)(2,1)S(1)}, bf16[6,128,512]{2,1,0:T(8,128)(2,1)}, u32[]{:S(2)}) copy-start(bf16[6,128,512]{2,1,0:T(8,128)(2,1)} %param.4) | copy-start | bytes 2359300
Sparse Core Ops, SparseCore 0:
  11.7 84.2 reduce-scatter.1
  99.0 48.0 all-gather.12
  150.2 108.2 all-reduce.1
  262.6 162.1 all-gather.14
  439.9 158.8 all-gather.16
  612.0 158.8 all-gather.18
  773.9 48.4 all-gather.10
  824.9 158.5 all-gather.20
